TPU v7x, 32 devices: a whole 2x2x4 slice. The times are simulated.
32 devices in a mesh: tm: 8 (over y, x, core), space: 4 (over z).
Axes of the slice: x: 2, y: 2, z: 4, core: 2. Of those that a mesh axis runs over, the one named last changes fastest.
Arguments:
- node_fields: float32 [8, 5, 32, 128, 128], P('tm', None, 'space'), may hold values from -6 to 6
- region_label: int32 [32, 128, 128], P('space'), may hold values from 0 to 3
- sheet_shift: int32 [8, 128], P('tm'), may hold values from 0 to 1
- diffusivity: float32 [4], replicated, may hold values from 0.02 to 0.15
Outputs:
- updated_nodes: float32 [8, 5, 32, 128, 128], P('tm', None, 'space')
All inputs are finite; a program needn't handle non-finite values.
Results may differ from a plain program's by a relative error of at most 0.00002.
Values sent between devices are 32-bit elements; how exact they have to be, the bound alone decides.
A program may use at most 64 MiB of HBM per device.

v0:
```python
import math

import jax
import jax.numpy as jnp
import numpy as np
from jax import lax
from jax.sharding import PartitionSpec as P

NODES = 5
FINE_SWEEPS = 2


slice_length = 1.0


def with_halo(block, sides, width):
    for axis, dim in sides:
        count = lax.axis_size(axis)
        forward = [(i, i + 1) for i in range(count - 1)]
        backward = [(target, source) for source, target in forward]
        low = lax.ppermute(
            lax.slice_in_dim(block, block.shape[dim] - width, None, axis=dim), axis, forward
        )
        high = lax.ppermute(lax.slice_in_dim(block, 0, width, axis=dim), axis, backward)
        block = jnp.concatenate([low, block, high], axis=dim)
    return block


def from_behind(value, axis, by):
    peers = lax.axis_size(axis)
    pairs = [(i, i + by) for i in range(peers) if 0 <= i + by < peers]
    return lax.ppermute(value, axis, pairs)


def node_tables():
    radius = math.sqrt(3.0 / 7.0)
    points = [0.0, (1.0 - radius) / 2.0, 0.5, (1.0 + radius) / 2.0, 1.0]
    integrals = np.zeros((4, 5))
    for column in range(5):
        coeffs = [1.0]
        divisor = 1.0
        for other in range(5):
            if other != column:
                anchor = points[other]
                product = [0.0] * (len(coeffs) + 1)
                for degree in range(len(coeffs)):
                    product[degree + 1] = product[degree + 1] + coeffs[degree]
                    product[degree] = product[degree] - anchor * coeffs[degree]
                coeffs = product
                divisor = divisor * (points[column] - anchor)
        for row in range(4):
            bottom = points[row]
            summit = points[row + 1]
            amount = 0.0
            for degree in range(len(coeffs)):
                amount = amount + coeffs[degree] / (degree + 1) * (
                    summit ** (degree + 1) - bottom ** (degree + 1)
                )
            integrals[row, column] = amount / divisor
    return (np.array(points), integrals)


def combine(coefficients, stack):
    total = float(coefficients[0]) * stack[0]
    for index in range(1, len(coefficients)):
        total = total + float(coefficients[index]) * stack[index]
    return total


def lookup(labels, table):
    result = jnp.zeros(labels.shape, jnp.float32)
    for region in range(table.shape[0]):
        result = result + jnp.where(labels == region, table[region], 0.0)
    return result


def restrict(field):
    shape = field.shape
    blocks = field.reshape(shape[:-3] + (shape[-3] // 4, 4, shape[-2] // 2, 2, shape[-1]))
    return jnp.mean(blocks, axis=(-4, -2))


def prolong(coarse):
    return jnp.repeat(jnp.repeat(coarse, 4, axis=-3), 2, axis=-2)


def pad_rows(field):
    return jnp.pad(field, [(0, 0)] * (field.ndim - 3) + [(1, 1), (0, 0), (0, 0)])


def fine_rims(stack):
    return with_halo(stack, (("space", 1),), 1)


def neighbours(padded):
    center = padded[..., 1:-1, :, :]
    vertical = padded[..., 2:, :, :] + padded[..., :-2, :, :]
    across = jnp.roll(center, 1, -2) + jnp.roll(center, -1, -2)
    sideways = jnp.pad(center, [(0, 0)] * (center.ndim - 1) + [(1, 1)])
    lateral = sideways[..., 2:] + sideways[..., :-2]
    return (center, vertical, across, lateral)


def fine_rate(padded, kappa, advect):
    center, vertical, across, lateral = neighbours(padded)
    diffusion = kappa * (vertical + across + lateral - 6.0 * center)
    return diffusion - advect * (center - jnp.roll(center, 1, -2))


def coarse_rate(padded, kappa, advect):
    center, vertical, across, lateral = neighbours(padded)
    diffusion = kappa * (
        (vertical - 2.0 * center) / 16.0 + (across - 2.0 * center) / 4.0 + (lateral - 2.0 * center)
    )
    return diffusion - 0.5 * advect * (center - jnp.roll(center, 1, -2))


def coarse_advance(initial, padded, kappa, advect, constant):
    return initial + slice_length * coarse_rate(padded, kappa, advect) + constant


def apply_correction(fields, delta_start, delta_end):
    times_table, integral_table = node_tables()
    pieces = []
    for node in range(NODES):
        weight = float(times_table[node])
        pieces.append(fields[node] + prolong((1.0 - weight) * delta_start + weight * delta_end))
    return jnp.stack(pieces)


def fine_sweeps(corrected, rates, kappa, advect, rims):
    times_table, integral_table = node_tables()
    old_values, old_rates = (corrected, rates)
    for sweep in range(FINE_SWEEPS):
        values = [old_values[0]]
        new_rates = [old_rates[0]]
        for node in range(NODES - 1):
            spacing = float(times_table[node + 1] - times_table[node]) * slice_length
            value = (
                values[node]
                + spacing * (new_rates[node] - old_rates[node])
                + slice_length * combine(integral_table[node], old_rates)
            )
            values.append(value)
            if node < NODES - 2 or sweep < FINE_SWEEPS - 1:
                new_rates.append(fine_rate(rims(value[None]), kappa, advect)[0])
        old_values = jnp.stack(values)
        if sweep < FINE_SWEEPS - 1:
            old_rates = jnp.stack(new_rates)
    return old_values


def shards(node_fields, region_label, sheet_shift, diffusivity):
    times_table, integral_table = node_tables()
    weight_table = integral_table.sum(axis=0)
    fields = node_fields[0]
    kappa = lookup(region_label, diffusivity)
    kappa_coarse = restrict(kappa)
    advect = sheet_shift[0].astype(jnp.float32) / slice_length
    first = lax.axis_index("tm") == 0
    arrived = from_behind(fields[NODES - 1], "tm", 1)
    start = jnp.where(first, fields[0], arrived)
    fields = jnp.concatenate([start[None], fields[1:]], 0)
    rates = fine_rate(fine_rims(fields), kappa, advect)
    coarse_start = restrict(start)
    coarse_end = restrict(fields[NODES - 1])
    moved = restrict(slice_length * combine(weight_table, rates))
    whole_start, whole_moved, whole_kappa = (
        lax.all_gather(coarse_start, "space", axis=0, tiled=True),
        lax.all_gather(moved, "space", axis=0, tiled=True),
        lax.all_gather(kappa_coarse, "space", axis=0, tiled=True),
    )
    constant = whole_moved - slice_length * coarse_rate(pad_rows(whole_start), whole_kappa, advect)

    def advance_whole(initial):
        return coarse_advance(initial, pad_rows(initial), whole_kappa, advect, constant)

    def turn_whole(index, carry):
        received = from_behind(carry[1], "tm", 1)
        begin_value = jnp.where(first, whole_start, received)
        return (begin_value, advance_whole(begin_value))

    whole_begin, whole_end = lax.fori_loop(
        0, lax.axis_size("tm") - 1, turn_whole, (whole_start, advance_whole(whole_start))
    )
    rows = coarse_start.shape[0]
    offset = lax.axis_index("space") * rows
    begin = lax.dynamic_slice_in_dim(whole_begin, offset, rows, 0)
    ending = lax.dynamic_slice_in_dim(whole_end, offset, rows, 0)
    corrected = apply_correction(fields, begin - coarse_start, ending - coarse_end)
    corrected_rates = fine_rate(fine_rims(corrected), kappa, advect)
    result = fine_sweeps(corrected, corrected_rates, kappa, advect, fine_rims)
    return result[None]


def solution(mesh):
    in_specs = (P("tm", None, "space", None, None), P("space", None, None), P("tm", None), P())
    out_specs = P("tm", None, "space", None, None)
    return jax.shard_map(shards, mesh=mesh, in_specs=in_specs, out_specs=out_specs, check_vma=False)
```

profile of v0, /device:TPU:28, one launch (start us, length us, event | category | flops | bytes accessed | tf_op | source)
XLA Modules:
  0.0 244.6 jit_solution(10045251692610109339)
XLA Ops:
  6.0 3.9 %select_add_fusion = f32[8,128,128]{2,1,0:T(8,128)S(1)} fusion(s32[8,128,128]{2,1,0:T(8,128)} %param.7, f32[]{:T(128)} %bitcast.6, f32[]{:T(128)} %bitcast.5, f32[]{:T(128)} %bitcast.4, f32[]{:T(128)} %bitcast.3), kind=kLoop, calls=%fused_computation.218 | loop fusion | flops 1441792 | bytes 1048592 | tf_op jit(solution)/shard_map/add | solution.py:73
  10.1 14.5 %all_gather.10 = f32[8,64,128]{2,1,0:T(8,128)S(1)} all-gather(f32[2,64,128]{2,1,0:T(8,128)S(1)} %broadcast_multiply_fusion.2), channel_id=1, replica_groups=mesh['tm'=8,'space'=4] {'space'}, dimensions={0}, use_global_device_ids=true | all-gather | bytes 327680 | tf_op jit(solution)/shard_map/all_gather | solution.py:171
  30.7 14.2 %all_gather.9 = f32[8,64,128]{2,1,0:T(8,128)S(1)} all-gather(f32[2,64,128]{2,1,0:T(8,128)S(1)} %broadcast_multiply_fusion.3), channel_id=1, replica_groups=mesh['tm'=8,'space'=4] {'space'}, dimensions={0}, use_global_device_ids=true | all-gather | bytes 327680 | tf_op jit(solution)/shard_map/all_gather | solution.py:169
  52.6 4.3 %collective-permute-done.3 = f32[5,1,128,128]{3,2,1,0:T(8,128)S(1)} collective-permute-done((f32[5,1,128,128]{3,2,1,0:T(8,128)}, f32[5,1,128,128]{3,2,1,0:T(8,128)S(1)}, u32[]{:S(2)}, u32[]{:S(2)}) %collective-permute-start.3) | collective-permute-done | bytes 327712 | tf_op jit(solution)/shard_map/ppermute | solution.py:21
  60.0 14.3 %all_gather.11 = f32[8,64,128]{2,1,0:T(8,128)S(1)} all-gather(f32[2,64,128]{2,1,0:T(8,128)S(1)} %broadcast_multiply_fusion.1), channel_id=1, replica_groups=mesh['tm'=8,'space'=4] {'space'}, dimensions={0}, use_global_device_ids=true | all-gather | bytes 327680 | tf_op jit(solution)/shard_map/all_gather | solution.py:170
  74.5 65.2 %while.14 = (s32[]{:T(128)}, f32[8,64,128]{2,1,0:T(8,128)}, f32[8,64,128]{2,1,0:T(8,128)S(1)}, pred[]{:T(512)}, f32[8,64,128]{2,1,0:T(8,128)S(1)}, /*index=5*/f3...) while((s32[]{:T(128)}, f32[8,64,128]{2,1,0:T(8,128)}, ...), condition=%wide.region_4.5_spmd, body=%wide.region_3.4_spmd.sunk | while | flops 1310850 | bytes 5506722 | solution.py:183
  76.5 6.7 %collective-permute-done = f32[8,64,128]{2,1,0:T(8,128)S(1)} collective-permute-done((f32[8,64,128]{2,1,0:T(8,128)S(1)}, f32[8,64,128]{2,1,0:T(8,128)S(1)}, u32[]{:S(2)}, u32[]{:S(2)}) %collective-permute-start) | collective-permute-done | bytes 262176 | tf_op jit(solution)/shard_map/while/body/eval_jaxpr/ppermute | solution.py:32
  85.8 6.7 %collective-permute-done = f32[8,64,128]{2,1,0:T(8,128)S(1)} collective-permute-done((f32[8,64,128]{2,1,0:T(8,128)S(1)}, f32[8,64,128]{2,1,0:T(8,128)S(1)}, u32[]{:S(2)}, u32[]{:S(2)}) %collective-permute-start) | collective-permute-done | bytes 262176 | tf_op jit(solution)/shard_map/while/body/eval_jaxpr/ppermute | solution.py:32
  95.1 6.7 %collective-permute-done = f32[8,64,128]{2,1,0:T(8,128)S(1)} collective-permute-done((f32[8,64,128]{2,1,0:T(8,128)S(1)}, f32[8,64,128]{2,1,0:T(8,128)S(1)}, u32[]{:S(2)}, u32[]{:S(2)}) %collective-permute-start) | collective-permute-done | bytes 262176 | tf_op jit(solution)/shard_map/while/body/eval_jaxpr/ppermute | solution.py:32
  104.4 6.7 %collective-permute-done = f32[8,64,128]{2,1,0:T(8,128)S(1)} collective-permute-done((f32[8,64,128]{2,1,0:T(8,128)S(1)}, f32[8,64,128]{2,1,0:T(8,128)S(1)}, u32[]{:S(2)}, u32[]{:S(2)}) %collective-permute-start) | collective-permute-done | bytes 262176 | tf_op jit(solution)/shard_map/while/body/eval_jaxpr/ppermute | solution.py:32
  113.7 6.7 %collective-permute-done = f32[8,64,128]{2,1,0:T(8,128)S(1)} collective-permute-done((f32[8,64,128]{2,1,0:T(8,128)S(1)}, f32[8,64,128]{2,1,0:T(8,128)S(1)}, u32[]{:S(2)}, u32[]{:S(2)}) %collective-permute-start) | collective-permute-done | bytes 262176 | tf_op jit(solution)/shard_map/while/body/eval_jaxpr/ppermute | solution.py:32
  123.1 6.7 %collective-permute-done = f32[8,64,128]{2,1,0:T(8,128)S(1)} collective-permute-done((f32[8,64,128]{2,1,0:T(8,128)S(1)}, f32[8,64,128]{2,1,0:T(8,128)S(1)}, u32[]{:S(2)}, u32[]{:S(2)}) %collective-permute-start) | collective-permute-done | bytes 262176 | tf_op jit(solution)/shard_map/while/body/eval_jaxpr/ppermute | solution.py:32
  132.4 6.7 %collective-permute-done = f32[8,64,128]{2,1,0:T(8,128)S(1)} collective-permute-done((f32[8,64,128]{2,1,0:T(8,128)S(1)}, f32[8,64,128]{2,1,0:T(8,128)S(1)}, u32[]{:S(2)}, u32[]{:S(2)}) %collective-permute-start) | collective-permute-done | bytes 262176 | tf_op jit(solution)/shard_map/while/body/eval_jaxpr/ppermute | solution.py:32
  150.1 4.6 %collective-permute-done.5 = f32[5,1,128,128]{3,2,1,0:T(8,128)S(1)} collective-permute-done((f32[5,1,128,128]{3,2,1,0:T(8,128)S(1)}, f32[5,1,128,128]{3,2,1,0:T(8,128)S(1)}, u32[]{:S(2)}, u32[]{:S(2)}) %collective-permute-start.5) | collective-permute-done | bytes 327712 | tf_op jit(solution)/shard_map/ppermute | solution.py:21
  162.8 4.3 %collective-permute-done.7 = f32[1,1,128,128]{3,2,1,0:T(8,128)S(1)} collective-permute-done((f32[1,1,128,128]{3,2,1,0:T(8,128)S(1)}, f32[1,1,128,128]{3,2,1,0:T(8,128)S(1)}, u32[]{:S(2)}, u32[]{:S(2)}) %collective-permute-start.7) | collective-permute-done | bytes 65568 | tf_op jit(solution)/shard_map/ppermute | solution.py:21
  167.1 3.5 %bitcast_add_fusion.5 = (f32[8,128,128]{2,1,0:T(8,128)S(1)}, f32[1,8,128,128]{3,2,1,0:T(8,128)S(1)}) fusion(f32[8,128,128]{2,1,0:T(8,128)S(1)} %bitcast_add_fusion.7, f32[5,8,128,128]{3,2,1,0:T(8,128)S(1)} %fusion.23, f32[8,127,128]{2,1,0:T(8,128)S(1)} %get-tuple-element.213, f32[8,1,128]{2,1,0:T(1,128)S(1)} %get-tuple-element.210, ...), kind=kLoop, calls=%fused_computation.203 | loop fusion | flops 5242880 | bytes 6947344 | tf_op jit(solution)/shard_map/add | solution.py:140
  170.7 3.6 %collective-permute-start.8 = (f32[1,1,128,128]{3,2,1,0:T(8,128)S(1)}, f32[1,1,128,128]{3,2,1,0:T(8,128)S(1)}, u32[]{:S(2)}, u32[]{:S(2)}) collective-permute-start(f32[1,1,128,128]{3,2,1,0:T(8,128)S(1)} %get-tuple-element.199), channel_id=1, source_target_pairs={{1,0},{2,1},{3,2},{5,4},{6,5},{7,6},{9,8},{10,9},{11,10},{13,12},{... | collective-permute-start | bytes 196616 | tf_op jit(solution)/shard_map/ppermute | solution.py:24
  176.2 4.3 %collective-permute-done.9 = f32[1,1,128,128]{3,2,1,0:T(8,128)S(1)} collective-permute-done((f32[1,1,128,128]{3,2,1,0:T(8,128)S(1)}, f32[1,1,128,128]{3,2,1,0:T(8,128)S(1)}, u32[]{:S(2)}, u32[]{:S(2)}) %collective-permute-start.9) | collective-permute-done | bytes 65568 | tf_op jit(solution)/shard_map/ppermute | solution.py:21
  180.4 3.5 %bitcast_add_fusion.3 = (f32[8,128,128]{2,1,0:T(8,128)S(1)}, f32[1,8,128,128]{3,2,1,0:T(8,128)S(1)}) fusion(f32[8,128,128]{2,1,0:T(8,128)S(1)} %get-tuple-element.132, f32[5,8,128,128]{3,2,1,0:T(8,128)S(1)} %fusion.23, f32[8,127,128]{2,1,0:T(8,128)S(1)} %get-tuple-element.205, f32[8,1,128]{2,1,0:T(1,128)S(1)} %get-tuple-element.202, ...), kind=kLoop, calls=%fused_computation.201 | loop fusion | flops 5242880 | bytes 6947344 | tf_op jit(solution)/shard_map/add | solution.py:140
  187.9 4.7 %collective-permute-done.11 = f32[1,1,128,128]{3,2,1,0:T(8,128)S(1)} collective-permute-done((f32[1,1,128,128]{3,2,1,0:T(8,128)S(1)}, f32[1,1,128,128]{3,2,1,0:T(8,128)S(1)}, u32[]{:S(2)}, u32[]{:S(2)}) %collective-permute-start.11) | collective-permute-done | bytes 65568 | tf_op jit(solution)/shard_map/ppermute | solution.py:21
  199.9 4.1 %collective-permute-done.13 = f32[1,1,128,128]{3,2,1,0:T(8,128)S(1)} collective-permute-done((f32[1,1,128,128]{3,2,1,0:T(8,128)S(1)}, f32[1,1,128,128]{3,2,1,0:T(8,128)S(1)}, u32[]{:S(2)}, u32[]{:S(2)}) %collective-permute-start.13) | collective-permute-done | bytes 65568 | tf_op jit(solution)/shard_map/ppermute | solution.py:21
  211.8 4.3 %collective-permute-done.15 = f32[1,1,128,128]{3,2,1,0:T(8,128)S(1)} collective-permute-done((f32[1,1,128,128]{3,2,1,0:T(8,128)S(1)}, f32[1,1,128,128]{3,2,1,0:T(8,128)S(1)}, u32[]{:S(2)}, u32[]{:S(2)}) %collective-permute-start.15) | collective-permute-done | bytes 65568 | tf_op jit(solution)/shard_map/ppermute | solution.py:21
  223.7 4.3 %collective-permute-done.17 = f32[1,1,128,128]{3,2,1,0:T(8,128)S(1)} collective-permute-done((f32[1,1,128,128]{3,2,1,0:T(8,128)S(1)}, f32[1,1,128,128]{3,2,1,0:T(8,128)S(1)}, u32[]{:S(2)}, u32[]{:S(2)}) %collective-permute-start.17) | collective-permute-done | bytes 65568 | tf_op jit(solution)/shard_map/ppermute | solution.py:21
  235.4 4.3 %collective-permute-done.19 = f32[1,1,128,128]{3,2,1,0:T(8,128)S(1)} collective-permute-done((f32[1,1,128,128]{3,2,1,0:T(8,128)S(1)}, f32[1,1,128,128]{3,2,1,0:T(8,128)S(1)}, u32[]{:S(2)}, u32[]{:S(2)}) %collective-permute-start.19) | collective-permute-done | bytes 65568 | tf_op jit(solution)/shard_map/ppermute | solution.py:21
  (174 shorter events, 100.7 us)
Async XLA Ops:
  2.0 24.7 %collective-permute-start.1 = (f32[8,128,128]{2,1,0:T(8,128)}, f32[8,128,128]{2,1,0:T(8,128)}, u32[]{:S(2)}, u32[]{:S(2)}) collective-permute-start(f32[8,128,128]{2,1,0:T(8,128)} %get-tuple-element.158), channel_id=1, source_target_pairs={{0,4},{4,8},{8,12},{12,16},{16,20},{20,24},{24,28},{1,5},{5,9},{9,... | collective-permute-start | bytes 1572872 | tf_op jit(solution)/shard_map/ppermute | solution.py:32
  46.4 6.2 %collective-permute-start.2 = (f32[5,1,128,128]{3,2,1,0:T(8,128)}, f32[5,1,128,128]{3,2,1,0:T(8,128)S(1)}, u32[]{:S(2)}, u32[]{:S(2)}) collective-permute-start(f32[5,1,128,128]{3,2,1,0:T(8,128)} %get-tuple-element.155), channel_id=1, source_target_pairs={{1,0},{2,1},{3,2},{5,4},{6,5},{7,6},{9,8},{10,9},{11,10},{13,12},{... | collective-permute-start | bytes 983048 | tf_op jit(solution)/shard_map/ppermute | solution.py:24
  47.7 9.2 %collective-permute-start.3 = (f32[5,1,128,128]{3,2,1,0:T(8,128)}, f32[5,1,128,128]{3,2,1,0:T(8,128)S(1)}, u32[]{:S(2)}, u32[]{:S(2)}) collective-permute-start(f32[5,1,128,128]{3,2,1,0:T(8,128)} %get-tuple-element.156), channel_id=1, source_target_pairs={{0,1},{1,2},{2,3},{4,5},{5,6},{6,7},{8,9},{9,10},{10,11},{12,13},{... | collective-permute-start | bytes 983048 | tf_op jit(solution)/shard_map/ppermute | solution.py:21
  74.6 8.6 %collective-permute-start = (f32[8,64,128]{2,1,0:T(8,128)S(1)}, f32[8,64,128]{2,1,0:T(8,128)S(1)}, u32[]{:S(2)}, u32[]{:S(2)}) collective-permute-start(f32[8,64,128]{2,1,0:T(8,128)S(1)} %get-tuple-element.293), channel_id=1, source_target_pairs={{0,4},{4,8},{8,12},{12,16},{16,20},{20,24},{24,28},{1,5},{5,9},{9,... | collective-permute-start | bytes 786440 | tf_op jit(solution)/shard_map/while/body/eval_jaxpr/ppermute | solution.py:32
  83.9 8.6 %collective-permute-start = (f32[8,64,128]{2,1,0:T(8,128)S(1)}, f32[8,64,128]{2,1,0:T(8,128)S(1)}, u32[]{:S(2)}, u32[]{:S(2)}) collective-permute-start(f32[8,64,128]{2,1,0:T(8,128)S(1)} %get-tuple-element.293), channel_id=1, source_target_pairs={{0,4},{4,8},{8,12},{12,16},{16,20},{20,24},{24,28},{1,5},{5,9},{9,... | collective-permute-start | bytes 786440 | tf_op jit(solution)/shard_map/while/body/eval_jaxpr/ppermute | solution.py:32
  93.2 8.6 %collective-permute-start = (f32[8,64,128]{2,1,0:T(8,128)S(1)}, f32[8,64,128]{2,1,0:T(8,128)S(1)}, u32[]{:S(2)}, u32[]{:S(2)}) collective-permute-start(f32[8,64,128]{2,1,0:T(8,128)S(1)} %get-tuple-element.293), channel_id=1, source_target_pairs={{0,4},{4,8},{8,12},{12,16},{16,20},{20,24},{24,28},{1,5},{5,9},{9,... | collective-permute-start | bytes 786440 | tf_op jit(solution)/shard_map/while/body/eval_jaxpr/ppermute | solution.py:32
  102.5 8.6 %collective-permute-start = (f32[8,64,128]{2,1,0:T(8,128)S(1)}, f32[8,64,128]{2,1,0:T(8,128)S(1)}, u32[]{:S(2)}, u32[]{:S(2)}) collective-permute-start(f32[8,64,128]{2,1,0:T(8,128)S(1)} %get-tuple-element.293), channel_id=1, source_target_pairs={{0,4},{4,8},{8,12},{12,16},{16,20},{20,24},{24,28},{1,5},{5,9},{9,... | collective-permute-start | bytes 786440 | tf_op jit(solution)/shard_map/while/body/eval_jaxpr/ppermute | solution.py:32
  111.8 8.6 %collective-permute-start = (f32[8,64,128]{2,1,0:T(8,128)S(1)}, f32[8,64,128]{2,1,0:T(8,128)S(1)}, u32[]{:S(2)}, u32[]{:S(2)}) collective-permute-start(f32[8,64,128]{2,1,0:T(8,128)S(1)} %get-tuple-element.293), channel_id=1, source_target_pairs={{0,4},{4,8},{8,12},{12,16},{16,20},{20,24},{24,28},{1,5},{5,9},{9,... | collective-permute-start | bytes 786440 | tf_op jit(solution)/shard_map/while/body/eval_jaxpr/ppermute | solution.py:32
  121.1 8.6 %collective-permute-start = (f32[8,64,128]{2,1,0:T(8,128)S(1)}, f32[8,64,128]{2,1,0:T(8,128)S(1)}, u32[]{:S(2)}, u32[]{:S(2)}) collective-permute-start(f32[8,64,128]{2,1,0:T(8,128)S(1)} %get-tuple-element.293), channel_id=1, source_target_pairs={{0,4},{4,8},{8,12},{12,16},{16,20},{20,24},{24,28},{1,5},{5,9},{9,... | collective-permute-start | bytes 786440 | tf_op jit(solution)/shard_map/while/body/eval_jaxpr/ppermute | solution.py:32
  130.4 8.6 %collective-permute-start = (f32[8,64,128]{2,1,0:T(8,128)S(1)}, f32[8,64,128]{2,1,0:T(8,128)S(1)}, u32[]{:S(2)}, u32[]{:S(2)}) collective-permute-start(f32[8,64,128]{2,1,0:T(8,128)S(1)} %get-tuple-element.293), channel_id=1, source_target_pairs={{0,4},{4,8},{8,12},{12,16},{16,20},{20,24},{24,28},{1,5},{5,9},{9,... | collective-permute-start | bytes 786440 | tf_op jit(solution)/shard_map/while/body/eval_jaxpr/ppermute | solution.py:32
  143.7 6.3 %collective-permute-start.4 = (f32[5,1,128,128]{3,2,1,0:T(8,128)S(1)}, f32[5,1,128,128]{3,2,1,0:T(8,128)S(1)}, u32[]{:S(2)}, u32[]{:S(2)}) collective-permute-start(f32[5,1,128,128]{3,2,1,0:T(8,128)S(1)} %get-tuple-element.149), channel_id=1, source_target_pairs={{1,0},{2,1},{3,2},{5,4},{6,5},{7,6},{9,8},{10,9},{11,10},{13,12},{... | collective-permute-start | bytes 983048 | tf_op jit(solution)/shard_map/ppermute | solution.py:24
  145.5 9.1 %collective-permute-start.5 = (f32[5,1,128,128]{3,2,1,0:T(8,128)S(1)}, f32[5,1,128,128]{3,2,1,0:T(8,128)S(1)}, u32[]{:S(2)}, u32[]{:S(2)}) collective-permute-start(f32[5,1,128,128]{3,2,1,0:T(8,128)S(1)} %get-tuple-element.150), channel_id=1, source_target_pairs={{0,1},{1,2},{2,3},{4,5},{5,6},{6,7},{8,9},{9,10},{10,11},{12,13},{... | collective-permute-start | bytes 983048 | tf_op jit(solution)/shard_map/ppermute | solution.py:21
  157.8 5.0 %collective-permute-start.6 = (f32[1,1,128,128]{3,2,1,0:T(8,128)S(1)}, f32[1,1,128,128]{3,2,1,0:T(8,128)S(1)}, u32[]{:S(2)}, u32[]{:S(2)}) collective-permute-start(f32[1,1,128,128]{3,2,1,0:T(8,128)S(1)} %get-tuple-element.207), channel_id=1, source_target_pairs={{1,0},{2,1},{3,2},{5,4},{6,5},{7,6},{9,8},{10,9},{11,10},{13,12},{... | collective-permute-start | bytes 196616 | tf_op jit(solution)/shard_map/ppermute | solution.py:24
  160.9 6.2 %collective-permute-start.7 = (f32[1,1,128,128]{3,2,1,0:T(8,128)S(1)}, f32[1,1,128,128]{3,2,1,0:T(8,128)S(1)}, u32[]{:S(2)}, u32[]{:S(2)}) collective-permute-start(f32[1,1,128,128]{3,2,1,0:T(8,128)S(1)} %get-tuple-element.208), channel_id=1, source_target_pairs={{0,1},{1,2},{2,3},{4,5},{5,6},{6,7},{8,9},{9,10},{10,11},{12,13},{... | collective-permute-start | bytes 196616 | tf_op jit(solution)/shard_map/ppermute | solution.py:21
  170.7 5.4 %collective-permute-start.8 = (f32[1,1,128,128]{3,2,1,0:T(8,128)S(1)}, f32[1,1,128,128]{3,2,1,0:T(8,128)S(1)}, u32[]{:S(2)}, u32[]{:S(2)}) collective-permute-start(f32[1,1,128,128]{3,2,1,0:T(8,128)S(1)} %get-tuple-element.199), channel_id=1, source_target_pairs={{1,0},{2,1},{3,2},{5,4},{6,5},{7,6},{9,8},{10,9},{11,10},{13,12},{... | collective-permute-start | bytes 196616 | tf_op jit(solution)/shard_map/ppermute | solution.py:24
  174.3 6.2 %collective-permute-start.9 = (f32[1,1,128,128]{3,2,1,0:T(8,128)S(1)}, f32[1,1,128,128]{3,2,1,0:T(8,128)S(1)}, u32[]{:S(2)}, u32[]{:S(2)}) collective-permute-start(f32[1,1,128,128]{3,2,1,0:T(8,128)S(1)} %get-tuple-element.200), channel_id=1, source_target_pairs={{0,1},{1,2},{2,3},{4,5},{5,6},{6,7},{8,9},{9,10},{10,11},{12,13},{... | collective-permute-start | bytes 196616 | tf_op jit(solution)/shard_map/ppermute | solution.py:21
  184.1 3.8 %collective-permute-start.10 = (f32[1,1,128,128]{3,2,1,0:T(8,128)S(1)}, f32[1,1,128,128]{3,2,1,0:T(8,128)S(1)}, u32[]{:S(2)}, u32[]{:S(2)}) collective-permute-start(f32[1,1,128,128]{3,2,1,0:T(8,128)S(1)} %get-tuple-element.191), channel_id=1, source_target_pairs={{1,0},{2,1},{3,2},{5,4},{6,5},{7,6},{9,8},{10,9},{11,10},{13,12},{... | collective-permute-start | bytes 196616 | tf_op jit(solution)/shard_map/ppermute | solution.py:24
  186.2 6.4 %collective-permute-start.11 = (f32[1,1,128,128]{3,2,1,0:T(8,128)S(1)}, f32[1,1,128,128]{3,2,1,0:T(8,128)S(1)}, u32[]{:S(2)}, u32[]{:S(2)}) collective-permute-start(f32[1,1,128,128]{3,2,1,0:T(8,128)S(1)} %get-tuple-element.192), channel_id=1, source_target_pairs={{0,1},{1,2},{2,3},{4,5},{5,6},{6,7},{8,9},{9,10},{10,11},{12,13},{... | collective-permute-start | bytes 196616 | tf_op jit(solution)/shard_map/ppermute | solution.py:21
  197.9 6.2 %collective-permute-start.13 = (f32[1,1,128,128]{3,2,1,0:T(8,128)S(1)}, f32[1,1,128,128]{3,2,1,0:T(8,128)S(1)}, u32[]{:S(2)}, u32[]{:S(2)}) collective-permute-start(f32[1,1,128,128]{3,2,1,0:T(8,128)S(1)} %get-tuple-element.184), channel_id=1, source_target_pairs={{0,1},{1,2},{2,3},{4,5},{5,6},{6,7},{8,9},{9,10},{10,11},{12,13},{... | collective-permute-start | bytes 196616 | tf_op jit(solution)/shard_map/ppermute | solution.py:21
  207.7 4.1 %collective-permute-start.14 = (f32[1,1,128,128]{3,2,1,0:T(8,128)S(1)}, f32[1,1,128,128]{3,2,1,0:T(8,128)S(1)}, u32[]{:S(2)}, u32[]{:S(2)}) collective-permute-start(f32[1,1,128,128]{3,2,1,0:T(8,128)S(1)} %get-tuple-element.175), channel_id=1, source_target_pairs={{1,0},{2,1},{3,2},{5,4},{6,5},{7,6},{9,8},{10,9},{11,10},{13,12},{... | collective-permute-start | bytes 196616 | tf_op jit(solution)/shard_map/ppermute | solution.py:24
  209.9 6.2 %collective-permute-start.15 = (f32[1,1,128,128]{3,2,1,0:T(8,128)S(1)}, f32[1,1,128,128]{3,2,1,0:T(8,128)S(1)}, u32[]{:S(2)}, u32[]{:S(2)}) collective-permute-start(f32[1,1,128,128]{3,2,1,0:T(8,128)S(1)} %get-tuple-element.176), channel_id=1, source_target_pairs={{0,1},{1,2},{2,3},{4,5},{5,6},{6,7},{8,9},{9,10},{10,11},{12,13},{... | collective-permute-start | bytes 196616 | tf_op jit(solution)/shard_map/ppermute | solution.py:21
  219.6 4.1 %collective-permute-start.16 = (f32[1,1,128,128]{3,2,1,0:T(8,128)S(1)}, f32[1,1,128,128]{3,2,1,0:T(8,128)S(1)}, u32[]{:S(2)}, u32[]{:S(2)}) collective-permute-start(f32[1,1,128,128]{3,2,1,0:T(8,128)S(1)} %get-tuple-element.167), channel_id=1, source_target_pairs={{1,0},{2,1},{3,2},{5,4},{6,5},{7,6},{9,8},{10,9},{11,10},{13,12},{... | collective-permute-start | bytes 196616 | tf_op jit(solution)/shard_map/ppermute | solution.py:24
  221.8 6.2 %collective-permute-start.17 = (f32[1,1,128,128]{3,2,1,0:T(8,128)S(1)}, f32[1,1,128,128]{3,2,1,0:T(8,128)S(1)}, u32[]{:S(2)}, u32[]{:S(2)}) collective-permute-start(f32[1,1,128,128]{3,2,1,0:T(8,128)S(1)} %get-tuple-element.168), channel_id=1, source_target_pairs={{0,1},{1,2},{2,3},{4,5},{5,6},{6,7},{8,9},{9,10},{10,11},{12,13},{... | collective-permute-start | bytes 196616 | tf_op jit(solution)/shard_map/ppermute | solution.py:21
  233.5 6.2 %collective-permute-start.19 = (f32[1,1,128,128]{3,2,1,0:T(8,128)S(1)}, f32[1,1,128,128]{3,2,1,0:T(8,128)S(1)}, u32[]{:S(2)}, u32[]{:S(2)}) collective-permute-start(f32[1,1,128,128]{3,2,1,0:T(8,128)S(1)} %get-tuple-element.166), channel_id=1, source_target_pairs={{0,1},{1,2},{2,3},{4,5},{5,6},{6,7},{8,9},{9,10},{10,11},{12,13},{... | collective-permute-start | bytes 196616 | tf_op jit(solution)/shard_map/ppermute | solution.py:21
  (18 other events, 106.5 us)
where the time goes:
time: 246 us; the launch traced here: 245 us
  waiting for transfers between devices  95 us (39%)
  starting transfers between devices  46.9 us (19%)
  other arithmetic  43.6 us (18%)
  blocking collectives  42.9 us (17%)
  local copies, waits for them, and re-layouts  15.2 us (6%)
    ppermute x8, waiting for transfers between devices, from_behind(): return lax.ppermute(value, axis, pairs)  46.6 us
    ppermute x9, waiting for transfers between devices, with_halo(): lax.ppermute(lax.slice_in_dim(block, block.shape[dim] - width, None, axis...  39 us
    ppermute x9, starting transfers between devices, with_halo(): lax.ppermute(lax.slice_in_dim(block, 0, width, axis=dim), axis, backward)  19.8 us
    ppermute x8, starting transfers between devices, from_behind(): return lax.ppermute(value, axis, pairs)  15.3 us
    all_gather x1, blocking collectives, shards(): lax.all_gather(kappa_coarse, 'space', axis=0, tiled=True)  14.5 us
    all_gather x1, blocking collectives, shards(): lax.all_gather(moved, 'space', axis=0, tiled=True)  14.3 us
    all_gather x1, blocking collectives, shards(): lax.all_gather(coarse_start, 'space', axis=0, tiled=True)  14.2 us
    ppermute x9, starting transfers between devices, with_halo(): lax.ppermute(lax.slice_in_dim(block, block.shape[dim] - width, None, axis...  11.8 us
  transfers between devices with their start and end apart: 26, of which 25 were waited for; matrix products, arithmetic and copies ran while one was open for 4% of the time, Pallas kernels for 0%

commit v1 on v0

v1 whole, which is shorter than its diff:
```python
import math

import jax
import jax.numpy as jnp
import numpy as np
from jax import lax
from jax.experimental import pallas as pl
from jax.experimental.pallas import tpu as pltpu
from jax.sharding import PartitionSpec as P

NODES = 5
FINE_SWEEPS = 2
BLOCK_Z = 4
BLOCK_X = 2
PAD = 8
MESH = pl.DeviceIdType.MESH

slice_length = 1.0


def node_tables():
    radius = math.sqrt(3.0 / 7.0)
    points = [0.0, (1.0 - radius) / 2.0, 0.5, (1.0 + radius) / 2.0, 1.0]
    integrals = np.zeros((4, 5))
    for column in range(5):
        coeffs = [1.0]
        divisor = 1.0
        for other in range(5):
            if other != column:
                anchor = points[other]
                product = [0.0] * (len(coeffs) + 1)
                for degree in range(len(coeffs)):
                    product[degree + 1] = product[degree + 1] + coeffs[degree]
                    product[degree] = product[degree] - anchor * coeffs[degree]
                coeffs = product
                divisor = divisor * (points[column] - anchor)
        for row in range(4):
            bottom = points[row]
            summit = points[row + 1]
            amount = 0.0
            for degree in range(len(coeffs)):
                amount = amount + coeffs[degree] / (degree + 1) * (
                    summit ** (degree + 1) - bottom ** (degree + 1)
                )
            integrals[row, column] = amount / divisor
    return (np.array(points), integrals)


TIMES, INTEGRALS = node_tables()
WEIGHTS = INTEGRALS.sum(axis=0)
STEPS = NODES - 1
EXCHANGES = 2 + FINE_SWEEPS * STEPS


class Transfer:
    def __init__(self, src, dst, send_sem, recv_sem, device, sends, receives):
        self.copy = pltpu.make_async_remote_copy(
            src_ref=src,
            dst_ref=dst,
            send_sem=send_sem,
            recv_sem=recv_sem,
            device_id=device,
            device_id_type=MESH,
        )
        self.sends, self.receives = sends, receives

    def start(self):
        pl.when(self.sends)(self.copy.start)

    def wait_recv(self):
        pl.when(self.receives)(self.copy.wait_recv)

    def wait_send(self):
        pl.when(self.sends)(self.copy.wait_send)


def kernel(
    fields, label, shift, table, out,
    kappa, kappa_c, start, moved, shift_next, below, pads, values, mids, spread, gain, lift, delta, ahead, fold,
    halo_send, halo_recv, time_send, time_recv,
):
    n, s = lax.axis_index("tm"), lax.axis_index("space")
    slices, slabs = lax.axis_size("tm"), lax.axis_size("space")
    depth, width, height = label.shape
    rows_c = width // BLOCK_X
    depth_c = depth // BLOCK_Z
    chunk = min(64, width)
    last = NODES - 1
    has_prev, has_next = n > 0, n < slices - 1
    has_low, has_high = s > 0, s < slabs - 1
    inner = pl.ds(PAD, width)

    barrier = pltpu.get_barrier_semaphore()
    met = jnp.int32(0)
    for dn in (-1, 0, 1):
        for ds in (-1, 0, 1):
            if dn == 0 and ds == 0:
                continue
            there = (n + dn >= 0) & (n + dn < slices) & (s + ds >= 0) & (s + ds < slabs)

            @pl.when(there)
            def _(dn=dn, ds=ds):
                pl.semaphore_signal(
                    barrier, inc=1, device_id={"tm": n + dn, "space": s + ds}, device_id_type=MESH
                )

            met = met + there.astype(jnp.int32)
    pl.semaphore_wait(barrier, met)

    shipped = []

    def send(transfer):
        transfer.start()
        shipped.append(transfer)
        return transfer

    def halo(index, low_src=None, high_src=None):
        buf = pads.at[index]
        low_src = buf.at[1, inner] if low_src is None else low_src
        high_src = buf.at[depth, inner] if high_src is None else high_src
        up = Transfer(
            high_src, buf.at[0, inner], halo_send.at[2 * index], halo_recv.at[2 * index],
            {"space": s + 1}, has_high, has_low,
        )
        down = Transfer(
            low_src, buf.at[depth + 1, inner], halo_send.at[2 * index + 1], halo_recv.at[2 * index + 1],
            {"space": s - 1}, has_low, has_high,
        )
        send(up)
        send(down)
        return (up, down)

    def arrive(pair):
        for transfer in pair:
            transfer.wait_recv()

    def time_hop(index, src, dst, ds=0):
        to = {"tm": n + 1} if ds == 0 else {"tm": n + 1, "space": s + ds}
        goes = has_next if ds == 0 else has_next & (s + ds >= 0) & (s + ds < slabs)
        comes = has_prev if ds == 0 else has_prev & (s - ds >= 0) & (s - ds < slabs)
        return Transfer(src, dst, time_send.at[index], time_recv.at[index], to, goes, comes)

    shift_hop = Transfer(
        shift, shift_next, time_send.at[0], time_recv.at[0], {"tm": n - 1}, has_prev, has_next
    )
    send(shift_hop)
    end_halo = halo(1, fields.at[last, 0], fields.at[last, depth - 1])
    start_hop = send(time_hop(1, fields.at[last], start))

    lane = lax.broadcasted_iota(jnp.int32, (chunk, height), 1)
    first_lane, last_lane = lane == 0, lane == height - 1
    lane_c = lax.broadcasted_iota(jnp.int32, (rows_c, height), 1)
    first_slice = (n == 0).astype(jnp.float32)

    def sideways(center, first, final):
        return jnp.where(final, 0.0, pltpu.roll(center, height - 1, 1)) + jnp.where(
            first, 0.0, pltpu.roll(center, 1, 1)
        )

    def rate(index, z, r, advect):
        center = pads[index, z + 1, pl.ds(PAD + r, chunk)]
        behind = pads[index, z + 1, pl.ds(PAD - 1 + r, chunk)]
        total = pads[index, z, pl.ds(PAD + r, chunk)] + pads[index, z + 2, pl.ds(PAD + r, chunk)]
        total = total + (behind + pads[index, z + 1, pl.ds(PAD + 1 + r, chunk)])
        total = total + sideways(center, first_lane, last_lane) - 6.0 * center
        return kappa[z, pl.ds(r, chunk)] * total - advect * (center - behind)

    def fill(index, z, r, value):
        pads[index, z + 1, pl.ds(PAD + r, chunk)] = value
        if r == 0:
            pads[index, z + 1, pl.ds(PAD + width, 1)] = value[:1]
        if r + chunk == width:
            pads[index, z + 1, pl.ds(PAD - 1, 1)] = value[chunk - 1 :]

    def each(lo, hi, body, place=lambda i: i):
        def turn(i, carry):
            z = place(i)
            for r in range(0, width, chunk):
                body(z, r)
            return carry

        lax.fori_loop(lo, hi, turn, 0)

    def edges(body):
        each(0, 2, body, lambda i: i * (depth - 1))

    def interior(body):
        each(1, depth - 1, body)

    def weigh(z, r):
        at = pl.ds(r, chunk)
        total = (first_slice * float(WEIGHTS[0])) * fields[0, z, at]
        for node in range(1, NODES):
            total = total + float(WEIGHTS[node]) * fields[node, z, at]
        fill(0, z, r, total)

    edges(weigh)
    weighted_halo = halo(0)
    interior(weigh)

    def prepare(z, r):
        at = pl.ds(r, chunk)
        fill(1, z, r, fields[last, z, at])
        labels = label[z, at]
        total = jnp.zeros((chunk, height), jnp.float32)
        for region in range(table.shape[0]):
            total = total + jnp.where(labels == region, table[region], 0.0)
        kappa[z, at] = total

    each(0, depth, prepare)

    for index in range(EXCHANGES):

        @pl.when(jnp.logical_not(has_low))
        def _(index=index):
            pads[index, 0, inner] = jnp.zeros((width, height), jnp.float32)

        @pl.when(jnp.logical_not(has_high))
        def _(index=index):
            pads[index, depth + 1, inner] = jnp.zeros((width, height), jnp.float32)

    def restrict(target, layer_of):
        def turn(zc, carry):
            for r in range(0, width, chunk):
                total = layer_of(BLOCK_Z * zc, r)
                for k in range(1, BLOCK_Z):
                    total = total + layer_of(BLOCK_Z * zc + k, r)
                fold[pl.ds(r, chunk)] = total
            total = fold[pl.ds(0, rows_c, stride=BLOCK_X)]
            for k in range(1, BLOCK_X):
                total = total + fold[pl.ds(k, rows_c, stride=BLOCK_X)]
            target[zc] = total * (1.0 / (BLOCK_Z * BLOCK_X))
            return carry

        lax.fori_loop(0, depth_c, turn, 0)

    advect = shift[...].astype(jnp.float32) / slice_length

    shift_hop.wait_recv()
    arrive(end_halo)
    advect_next = shift_next[...].astype(jnp.float32) / slice_length
    restrict(
        lift,
        lambda z, r: fields[last, z, pl.ds(r, chunk)]
        + (slice_length * float(WEIGHTS[0])) * rate(1, z, r, advect_next),
    )
    lift_hop = send(time_hop(2, lift, moved))

    restrict(kappa_c, lambda z, r: kappa[z, pl.ds(r, chunk)])
    arrive(weighted_halo)
    restrict(
        gain,
        lambda z, r: first_slice * fields[0, z, pl.ds(r, chunk)]
        - fields[last, z, pl.ds(r, chunk)]
        + slice_length * rate(0, z, r, advect),
    )

    @pl.when(jnp.logical_not(has_prev))
    def _():
        moved[...] = jnp.zeros_like(moved)
        delta[...] = jnp.zeros_like(delta)
        below[...] = jnp.zeros_like(below)

    @pl.when(has_prev & jnp.logical_not(has_low))
    def _():
        below[0] = jnp.zeros((rows_c, height), jnp.float32)

    @pl.when(has_prev & jnp.logical_not(has_high))
    def _():
        below[1] = jnp.zeros((rows_c, height), jnp.float32)

    body_hop = time_hop(3, ahead, delta)
    up_hop = time_hop(4, ahead.at[depth_c - 1], below.at[0], 1)
    down_hop = time_hop(5, ahead.at[0], below.at[1], -1)
    lift_hop.wait_recv()
    gain[...] = gain[...] + moved[...]
    body_hop.wait_recv()
    up_hop.wait_recv()
    down_hop.wait_recv()
    for zc in range(depth_c):
        center = delta[zc]
        under = below[0] if zc == 0 else delta[zc - 1]
        over = below[1] if zc == depth_c - 1 else delta[zc + 1]
        behind = pltpu.roll(center, 1, 0)
        across = behind + pltpu.roll(center, rows_c - 1, 0)
        lateral = sideways(center, lane_c == 0, lane_c == height - 1)
        spreading = kappa_c[zc] * (
            (under + over - 2.0 * center) * (1.0 / (BLOCK_Z * BLOCK_Z))
            + (across - 2.0 * center) * (1.0 / (BLOCK_X * BLOCK_X))
            + (lateral - 2.0 * center)
        )
        flow = (1.0 / BLOCK_X) * advect * (center - behind)
        ahead[zc] = center + slice_length * (spreading - flow) + gain[zc]
    send(body_hop)
    send(up_hop)
    send(down_hop)

    for zc in range(depth_c):
        for k in range(BLOCK_X):
            spread[0, zc, pl.ds(k, rows_c, stride=BLOCK_X)] = delta[zc]
            spread[1, zc, pl.ds(k, rows_c, stride=BLOCK_X)] = ahead[zc]

    start_hop.wait_recv()

    @pl.when(jnp.logical_not(has_prev))
    def _():
        def turn(z, carry):
            start[z] = fields[0, z]
            return carry

        lax.fori_loop(0, depth, turn, 0)

    def correct(z, r):
        at = pl.ds(r, chunk)
        zc = z // BLOCK_Z
        begin, ending = spread[0, zc, at], spread[1, zc, at]
        total = None
        for node in range(NODES):
            weight = float(TIMES[node])
            own = start[z, at] if node == 0 else fields[node, z, at]
            if node == 0:
                value = own + begin
                out[0, z, at] = value
            elif node == last:
                value = own + ending
            else:
                value = own + ((1.0 - weight) * begin + weight * ending)
            if node > 0:
                values[node - 1, z, at] = value
            term = (slice_length * float(INTEGRALS[0, node])) * value
            total = term if total is None else total + term
        fill(2, z, r, total)

    edges(correct)
    pair = halo(2)
    interior(correct)

    for sweep in range(FINE_SWEEPS):
        old = values if sweep == 0 else mids
        new = mids if sweep == 0 else None
        for step in range(STEPS):
            index = 2 + sweep * STEPS + step
            final = sweep == FINE_SWEEPS - 1
            more = not (final and step == STEPS - 1)

            def advance(z, r, index=index, step=step, old=old, new=new, final=final, more=more):
                at = pl.ds(r, chunk)
                if step == 0:
                    before = out[0, z, at]
                else:
                    before = out[step, z, at] if final else new[step - 1, z, at]
                value = before + rate(index, z, r, advect)
                if final:
                    out[step + 1, z, at] = value
                else:
                    new[step, z, at] = value
                if not more:
                    return
                if step < STEPS - 1:
                    gap = slice_length * float(TIMES[step + 2] - TIMES[step + 1])
                    total = gap * (value - old[step, z, at])
                    row, source, known = step + 1, old, {}
                else:
                    total, row, source, known = None, 0, new, {STEPS: value}
                for node in range(NODES):
                    if node == 0:
                        part = out[0, z, at]
                    else:
                        part = known[node] if node in known else source[node - 1, z, at]
                    term = (slice_length * float(INTEGRALS[row, node])) * part
                    total = term if total is None else total + term
                fill(index + 1, z, r, total)

            arrive(pair)
            edges(advance)
            if more:
                pair = halo(index + 1)
            interior(advance)

    for transfer in shipped:
        transfer.wait_send()


def shards(node_fields, region_label, sheet_shift, diffusivity):
    fields = node_fields[0]
    nodes, depth, width, height = fields.shape
    depth_c, rows_c = depth // BLOCK_Z, width // BLOCK_X
    f32 = jnp.float32
    fine = (depth, width, height)
    coarse = (depth_c, rows_c, height)
    vmem = pl.BlockSpec(memory_space=pltpu.VMEM)
    result = pl.pallas_call(
        kernel,
        out_shape=jax.ShapeDtypeStruct(fields.shape, f32),
        in_specs=[vmem, vmem, vmem, pl.BlockSpec(memory_space=pltpu.SMEM)],
        out_specs=vmem,
        scratch_shapes=[
            pltpu.VMEM(fine, f32),
            pltpu.VMEM(coarse, f32),
            pltpu.VMEM(fine, f32),
            pltpu.VMEM(coarse, f32),
            pltpu.VMEM(sheet_shift.shape, jnp.int32),
            pltpu.VMEM((2, rows_c, height), f32),
            pltpu.VMEM((EXCHANGES, depth + 2, width + 2 * PAD, height), f32),
            pltpu.VMEM((STEPS,) + fine, f32),
            pltpu.VMEM((STEPS,) + fine, f32),
            pltpu.VMEM((2, depth_c, width, height), f32),
            pltpu.VMEM(coarse, f32),
            pltpu.VMEM(coarse, f32),
            pltpu.VMEM(coarse, f32),
            pltpu.VMEM(coarse, f32),
            pltpu.VMEM((width, height), f32),
            pltpu.SemaphoreType.DMA((2 * EXCHANGES,)),
            pltpu.SemaphoreType.DMA((2 * EXCHANGES,)),
            pltpu.SemaphoreType.DMA((6,)),
            pltpu.SemaphoreType.DMA((6,)),
        ],
        compiler_params=pltpu.CompilerParams(
            collective_id=0, has_side_effects=True, vmem_limit_bytes=48 * 1024 * 1024
        ),
    )(fields, region_label, sheet_shift, diffusivity)
    return result[None]


def solution(mesh):
    in_specs = (P("tm", None, "space", None, None), P("space", None, None), P("tm", None), P())
    out_specs = P("tm", None, "space", None, None)
    return jax.shard_map(shards, mesh=mesh, in_specs=in_specs, out_specs=out_specs, check_vma=False)
```

time: 246 us -> 64.2 us (0.26)
  the two profiles are of different devices: /device:TPU:28 before, /device:TPU:6 now
where the time goes in v1:
time: 64.2 us; the launch traced here: 64 us
  Pallas kernels  58.4 us (91%)
  local copies, waits for them, and re-layouts  5.58 us (9%)
    pallas_call x1, Pallas kernels, shards(): pl.pallas_call(kernel, out_shape=jax.ShapeDtypeStruct(fields.shape, f32),...  58.4 us
    unnamed x9, local copies, waits for them, and re-layouts  5.58 us

profile of v1, /device:TPU:6, one launch (start us, length us, event | category | flops | bytes accessed | tf_op | source)
XLA Modules:
  0.0 64.0 jit_solution(10742389733873753318)
XLA Ops:
  0.0 0.0 copy-start
  0.0 1.7 %copy-done = f32[1,5,8,128,128]{4,3,2,1,0:T(8,128)S(1)} copy-done((f32[1,5,8,128,128]{4,3,2,1,0:T(8,128)S(1)}, f32[1,5,8,128,128]{4,3,2,1,0:T(8,128)}, u32[]{:S(2)}) %copy-start) | copy-done | bytes 2621464
  1.7 0.0 copy-start.1
  1.7 1.0 %copy-done.1 = s32[8,128,128]{2,1,0:T(8,128)S(1)} copy-done((s32[8,128,128]{2,1,0:T(8,128)S(1)}, s32[8,128,128]{2,1,0:T(8,128)}, u32[]{:S(2)}) %copy-start.1) | copy-done | bytes 524312
  2.8 0.0 copy-start.2
  2.8 0.7 %copy-done.2 = s32[1,128]{1,0:T(1,128)S(1)} copy-done((s32[1,128]{1,0:T(1,128)S(1)}, s32[1,128]{1,0:T(1,128)}, u32[]{:S(2)}) %copy-start.2) | copy-done | bytes 536
  3.4 0.0 copy-start.3
  3.4 0.7 %copy-done.3 = f32[4]{0:T(128)S(1)} copy-done((f32[4]{0:T(128)S(1)}, f32[4]{0:T(128)}, u32[]{:S(2)}) %copy-start.3) | copy-done | bytes 40
  4.1 58.4 %shard_map.46 = f32[5,8,128,128]{3,2,1,0:T(8,128)S(1)} custom-call(f32[5,8,128,128]{3,2,1,0:T(8,128)S(1)} %bitcast.3, s32[8,128,128]{2,1,0:T(8,128)S(1)} %copy-done.1, s32[1,128]{1,0:T(1,128)S(1)} %copy-done.2, f32[4]{0:T(128)S(1)} %copy-done.3), custom_call_target="tpu_custom_call" | custom-call | tf_op jit(solution)/shard_map/pallas_call | solution.py:392
  62.5 1.5 %copy.6 = f32[1,5,8,128,128]{4,3,2,1,0:T(8,128)} copy(f32[1,5,8,128,128]{4,3,2,1,0:T(8,128)S(1)} %bitcast.2) | data formatting | bytes 5242880
Async XLA Ops:
  0.0 1.7 %copy-start = (f32[1,5,8,128,128]{4,3,2,1,0:T(8,128)S(1)}, f32[1,5,8,128,128]{4,3,2,1,0:T(8,128)}, u32[]{:S(2)}) copy-start(f32[1,5,8,128,128]{4,3,2,1,0:T(8,128)} %param.4) | copy-start | bytes 7864324
  1.7 1.0 %copy-start.1 = (s32[8,128,128]{2,1,0:T(8,128)S(1)}, s32[8,128,128]{2,1,0:T(8,128)}, u32[]{:S(2)}) copy-start(s32[8,128,128]{2,1,0:T(8,128)} %label.1) | copy-start | bytes 1572868
  2.8 0.7 %copy-start.2 = (s32[1,128]{1,0:T(1,128)S(1)}, s32[1,128]{1,0:T(1,128)}, u32[]{:S(2)}) copy-start(s32[1,128]{1,0:T(1,128)} %shift.1) | copy-start | bytes 1540
  3.4 0.7 %copy-start.3 = (f32[4]{0:T(128)S(1)}, f32[4]{0:T(128)}, u32[]{:S(2)}) copy-start(f32[4]{0:T(128)} %table.1) | copy-start | bytes 52

commit v2 on v1

--- a/solution.py
+++ b/solution.py
@@ -13,6 +13,7 @@
 BLOCK_Z = 4
 BLOCK_X = 2
 PAD = 8
+PIECES = 4
 MESH = pl.DeviceIdType.MESH
 
 slice_length = 1.0
@@ -75,9 +76,9 @@
 
 
 def kernel(
-    fields, label, shift, table, out,
+    fields_in, label_in, shift_in, table_in, out, fields, label, shift, table,
     kappa, kappa_c, start, moved, shift_next, below, pads, values, mids, spread, gain, lift, delta, ahead, fold,
-    halo_send, halo_recv, time_send, time_recv,
+    halo_send, halo_recv, time_send, time_recv, load_sem,
 ):
     n, s = lax.axis_index("tm"), lax.axis_index("space")
     slices, slabs = lax.axis_size("tm"), lax.axis_size("space")
@@ -85,10 +86,23 @@
     rows_c = width // BLOCK_X
     depth_c = depth // BLOCK_Z
     chunk = min(64, width)
+    piece = width // PIECES
     last = NODES - 1
     has_prev, has_next = n > 0, n < slices - 1
     has_low, has_high = s > 0, s < slabs - 1
     inner = pl.ds(PAD, width)
+
+    loads = [
+        pltpu.make_async_copy(fields_in.at[node], fields.at[node], load_sem.at[node])
+        for node in range(NODES)
+    ]
+    loads += [
+        pltpu.make_async_copy(label_in, label, load_sem.at[NODES]),
+        pltpu.make_async_copy(shift_in, shift, load_sem.at[NODES + 1]),
+        pltpu.make_async_copy(table_in, table, load_sem.at[NODES + 2]),
+    ]
+    for load in loads:
+        load.start()
 
     barrier = pltpu.get_barrier_semaphore()
     met = jnp.int32(0)
@@ -114,25 +128,31 @@
         shipped.append(transfer)
         return transfer
 
-    def halo(index, low_src=None, high_src=None):
+    def halo(index, source=None):
         buf = pads.at[index]
-        low_src = buf.at[1, inner] if low_src is None else low_src
-        high_src = buf.at[depth, inner] if high_src is None else high_src
-        up = Transfer(
-            high_src, buf.at[0, inner], halo_send.at[2 * index], halo_recv.at[2 * index],
-            {"space": s + 1}, has_high, has_low,
-        )
-        down = Transfer(
-            low_src, buf.at[depth + 1, inner], halo_send.at[2 * index + 1], halo_recv.at[2 * index + 1],
-            {"space": s - 1}, has_low, has_high,
-        )
-        send(up)
-        send(down)
-        return (up, down)
-
-    def arrive(pair):
-        for transfer in pair:
-            transfer.wait_recv()
+        pieces = []
+        for k in range(PIECES):
+            rows = pl.ds(PAD + k * piece, piece)
+            if source is None:
+                low, high = buf.at[1, rows], buf.at[depth, rows]
+            else:
+                low, high = (source.at[z, pl.ds(k * piece, piece)] for z in (0, depth - 1))
+            sem = 2 * (index * PIECES + k)
+            up = Transfer(
+                high, buf.at[0, rows], halo_send.at[sem], halo_recv.at[sem],
+                {"space": s + 1}, has_high, has_low,
+            )
+            down = Transfer(
+                low, buf.at[depth + 1, rows], halo_send.at[sem + 1], halo_recv.at[sem + 1],
+                {"space": s - 1}, has_low, has_high,
+            )
+            pieces.append((down, up))
+        return pieces
+
+    def arrive(pieces):
+        for down, up in pieces:
+            down.wait_recv()
+            up.wait_recv()
 
     def time_hop(index, src, dst, ds=0):
         to = {"tm": n + 1} if ds == 0 else {"tm": n + 1, "space": s + ds}
@@ -141,64 +161,73 @@
         return Transfer(src, dst, time_send.at[index], time_recv.at[index], to, goes, comes)
 
     shift_hop = Transfer(
-        shift, shift_next, time_send.at[0], time_recv.at[0], {"tm": n - 1}, has_prev, has_next
+        shift_in, shift_next, time_send.at[0], time_recv.at[0], {"tm": n - 1}, has_prev, has_next
     )
     send(shift_hop)
-    end_halo = halo(1, fields.at[last, 0], fields.at[last, depth - 1])
-    start_hop = send(time_hop(1, fields.at[last], start))
-
-    lane = lax.broadcasted_iota(jnp.int32, (chunk, height), 1)
-    first_lane, last_lane = lane == 0, lane == height - 1
-    lane_c = lax.broadcasted_iota(jnp.int32, (rows_c, height), 1)
+    end_halo = halo(1, fields_in.at[last])
+    for down, up in end_halo:
+        send(down)
+        send(up)
+    start_hop = send(time_hop(1, fields_in.at[last], start))
+
     first_slice = (n == 0).astype(jnp.float32)
 
-    def sideways(center, first, final):
-        return jnp.where(final, 0.0, pltpu.roll(center, height - 1, 1)) + jnp.where(
-            first, 0.0, pltpu.roll(center, 1, 1)
+    def sideways(center):
+        lane = lax.broadcasted_iota(jnp.int32, center.shape, 1)
+        return jnp.where(lane == height - 1, 0.0, pltpu.roll(center, height - 1, 1)) + jnp.where(
+            lane == 0, 0.0, pltpu.roll(center, 1, 1)
         )
 
-    def rate(index, z, r, advect):
+    def rate(index, z, r, advect, chunk=chunk):
         center = pads[index, z + 1, pl.ds(PAD + r, chunk)]
         behind = pads[index, z + 1, pl.ds(PAD - 1 + r, chunk)]
         total = pads[index, z, pl.ds(PAD + r, chunk)] + pads[index, z + 2, pl.ds(PAD + r, chunk)]
         total = total + (behind + pads[index, z + 1, pl.ds(PAD + 1 + r, chunk)])
-        total = total + sideways(center, first_lane, last_lane) - 6.0 * center
+        total = total + sideways(center) - 6.0 * center
         return kappa[z, pl.ds(r, chunk)] * total - advect * (center - behind)
 
     def fill(index, z, r, value):
-        pads[index, z + 1, pl.ds(PAD + r, chunk)] = value
+        rows = value.shape[0]
+        pads[index, z + 1, pl.ds(PAD + r, rows)] = value
         if r == 0:
             pads[index, z + 1, pl.ds(PAD + width, 1)] = value[:1]
-        if r + chunk == width:
-            pads[index, z + 1, pl.ds(PAD - 1, 1)] = value[chunk - 1 :]
-
-    def each(lo, hi, body, place=lambda i: i):
-        def turn(i, carry):
-            z = place(i)
+        if r + rows == width:
+            pads[index, z + 1, pl.ds(PAD - 1, 1)] = value[rows - 1 :]
+
+    def each(lo, hi, body):
+        def turn(z, carry):
             for r in range(0, width, chunk):
-                body(z, r)
+                body(z, r, chunk)
             return carry
 
         lax.fori_loop(lo, hi, turn, 0)
 
-    def edges(body):
-        each(0, 2, body, lambda i: i * (depth - 1))
+    def edges(body, needs=None, gives=None):
+        for k in range(PIECES):
+            for side, z in ((0, 0), (1, depth - 1)):
+                if needs is not None:
+                    needs[k][1 - side].wait_recv()
+                body(z, k * piece, piece)
+                if gives is not None:
+                    send(gives[k][side])
 
     def interior(body):
         each(1, depth - 1, body)
 
-    def weigh(z, r):
+    def weigh(z, r, chunk):
         at = pl.ds(r, chunk)
         total = (first_slice * float(WEIGHTS[0])) * fields[0, z, at]
         for node in range(1, NODES):
             total = total + float(WEIGHTS[node]) * fields[node, z, at]
         fill(0, z, r, total)
 
-    edges(weigh)
+    for load in loads:
+        load.wait()
     weighted_halo = halo(0)
+    edges(weigh, None, weighted_halo)
     interior(weigh)
 
-    def prepare(z, r):
+    def prepare(z, r, chunk):
         at = pl.ds(r, chunk)
         fill(1, z, r, fields[last, z, at])
         labels = label[z, at]
@@ -283,7 +312,7 @@
         over = below[1] if zc == depth_c - 1 else delta[zc + 1]
         behind = pltpu.roll(center, 1, 0)
         across = behind + pltpu.roll(center, rows_c - 1, 0)
-        lateral = sideways(center, lane_c == 0, lane_c == height - 1)
+        lateral = sideways(center)
         spreading = kappa_c[zc] * (
             (under + over - 2.0 * center) * (1.0 / (BLOCK_Z * BLOCK_Z))
             + (across - 2.0 * center) * (1.0 / (BLOCK_X * BLOCK_X))
@@ -310,7 +339,7 @@
 
         lax.fori_loop(0, depth, turn, 0)
 
-    def correct(z, r):
+    def correct(z, r, chunk):
         at = pl.ds(r, chunk)
         zc = z // BLOCK_Z
         begin, ending = spread[0, zc, at], spread[1, zc, at]
@@ -331,8 +360,8 @@
             total = term if total is None else total + term
         fill(2, z, r, total)
 
-    edges(correct)
     pair = halo(2)
+    edges(correct, None, pair)
     interior(correct)
 
     for sweep in range(FINE_SWEEPS):
@@ -343,13 +372,13 @@
             final = sweep == FINE_SWEEPS - 1
             more = not (final and step == STEPS - 1)
 
-            def advance(z, r, index=index, step=step, old=old, new=new, final=final, more=more):
+            def advance(z, r, chunk, index=index, step=step, old=old, new=new, final=final, more=more):
                 at = pl.ds(r, chunk)
                 if step == 0:
                     before = out[0, z, at]
                 else:
                     before = out[step, z, at] if final else new[step - 1, z, at]
-                value = before + rate(index, z, r, advect)
+                value = before + rate(index, z, r, advect, chunk)
                 if final:
                     out[step + 1, z, at] = value
                 else:
@@ -371,11 +400,10 @@
                     total = term if total is None else total + term
                 fill(index + 1, z, r, total)
 
-            arrive(pair)
-            edges(advance)
-            if more:
-                pair = halo(index + 1)
+            following = halo(index + 1) if more else None
+            edges(advance, pair, following)
             interior(advance)
+            pair = following
 
     for transfer in shipped:
         transfer.wait_send()
@@ -388,13 +416,17 @@
     f32 = jnp.float32
     fine = (depth, width, height)
     coarse = (depth_c, rows_c, height)
-    vmem = pl.BlockSpec(memory_space=pltpu.VMEM)
+    vmem, hbm = (pl.BlockSpec(memory_space=space) for space in (pltpu.VMEM, pltpu.HBM))
     result = pl.pallas_call(
         kernel,
         out_shape=jax.ShapeDtypeStruct(fields.shape, f32),
-        in_specs=[vmem, vmem, vmem, pl.BlockSpec(memory_space=pltpu.SMEM)],
+        in_specs=[hbm] * 4,
         out_specs=vmem,
         scratch_shapes=[
+            pltpu.VMEM(fields.shape, f32),
+            pltpu.VMEM(fine, jnp.int32),
+            pltpu.VMEM(sheet_shift.shape, jnp.int32),
+            pltpu.SMEM(diffusivity.shape, f32),
             pltpu.VMEM(fine, f32),
             pltpu.VMEM(coarse, f32),
             pltpu.VMEM(fine, f32),
@@ -410,13 +442,14 @@
             pltpu.VMEM(coarse, f32),
             pltpu.VMEM(coarse, f32),
             pltpu.VMEM((width, height), f32),
-            pltpu.SemaphoreType.DMA((2 * EXCHANGES,)),
-            pltpu.SemaphoreType.DMA((2 * EXCHANGES,)),
+            pltpu.SemaphoreType.DMA((2 * EXCHANGES * PIECES,)),
+            pltpu.SemaphoreType.DMA((2 * EXCHANGES * PIECES,)),
             pltpu.SemaphoreType.DMA((6,)),
             pltpu.SemaphoreType.DMA((6,)),
+            pltpu.SemaphoreType.DMA((NODES + 3,)),
         ],
         compiler_params=pltpu.CompilerParams(
-            collective_id=0, has_side_effects=True, vmem_limit_bytes=48 * 1024 * 1024
+            collective_id=0, has_side_effects=True, vmem_limit_bytes=67043328
         ),
     )(fields, region_label, sheet_shift, diffusivity)
     return result[None]

time: 64.2 us -> 59.1 us (0.921)
  Pallas kernels: 58.4 us -> 55.4 us
  local copies, waits for them, and re-layouts: 5.58 us -> 3.53 us
    pallas_call x1, Pallas kernels: 58.4 us -> 55.4 us  [shards(): pl.pallas_call(kernel, out_shape=jax.ShapeDtypeStruct(fields.shape, f32),...]
    unnamed x9 -> x1, local copies, waits for them, and re-layouts: 5.58 us -> 3.53 us
where the time goes in v2:
time: 59.1 us; the launch traced here: 58.9 us
  Pallas kernels  55.4 us (94%)
  local copies, waits for them, and re-layouts  3.53 us (6%)
    pallas_call x1, Pallas kernels, shards(): pl.pallas_call(kernel, out_shape=jax.ShapeDtypeStruct(fields.shape, f32),...  55.4 us
    unnamed x1, local copies, waits for them, and re-layouts  3.53 us

profile of v2, /device:TPU:6, one launch (start us, length us, event | category | flops | bytes accessed | tf_op | source)
XLA Modules:
  0.0 58.9 jit_solution(5669769888643207141)
XLA Ops:
  0.0 55.4 %shard_map.46 = f32[5,8,128,128]{3,2,1,0:T(8,128)} custom-call(f32[5,8,128,128]{3,2,1,0:T(8,128)} %bitcast.3, s32[8,128,128]{2,1,0:T(8,128)} %label_in.1, s32[1,128]{1,0:T(1,128)} %shift_in.1, f32[4]{0:T(128)} %table_in.1), custom_call_target="tpu_custom_call" | custom-call | tf_op jit(solution)/shard_map/pallas_call | solution.py:420
  55.4 3.5 %copy.6 = f32[1,5,8,128,128]{4,3,2,1,0:T(8,128)} copy(f32[1,5,8,128,128]{4,3,2,1,0:T(8,128)} %bitcast.2) | data formatting | bytes 5242880

commit v3 on v2

--- a/solution.py
+++ b/solution.py
@@ -204,12 +204,13 @@
 
     def edges(body, needs=None, gives=None):
         for k in range(PIECES):
-            for side, z in ((0, 0), (1, depth - 1)):
-                if needs is not None:
-                    needs[k][1 - side].wait_recv()
-                body(z, k * piece, piece)
-                if gives is not None:
-                    send(gives[k][side])
+            if needs is not None:
+                arrive(needs[k : k + 1])
+            body(0, k * piece, piece)
+            body(depth - 1, k * piece, piece)
+            if gives is not None:
+                send(gives[k][0])
+                send(gives[k][1])
 
     def interior(body):
         each(1, depth - 1, body)
@@ -320,9 +321,11 @@
         )
         flow = (1.0 / BLOCK_X) * advect * (center - behind)
         ahead[zc] = center + slice_length * (spreading - flow) + gain[zc]
+        if zc == 0:
+            send(down_hop)
+        if zc == depth_c - 1:
+            send(up_hop)
     send(body_hop)
-    send(up_hop)
-    send(down_hop)
 
     for zc in range(depth_c):
         for k in range(BLOCK_X):
@@ -405,8 +408,15 @@
             interior(advance)
             pair = following
 
+    groups = {}
     for transfer in shipped:
-        transfer.wait_send()
+        groups.setdefault(id(transfer.sends), []).append(transfer)
+    for group in groups.values():
+
+        @pl.when(group[0].sends)
+        def _(group=group):
+            for transfer in group:
+                transfer.copy.wait_send()
 
 
 def shards(node_fields, region_label, sheet_shift, diffusivity):
@@ -449,9 +459,9 @@
             pltpu.SemaphoreType.DMA((NODES + 3,)),
         ],
         compiler_params=pltpu.CompilerParams(
-            collective_id=0, has_side_effects=True, vmem_limit_bytes=67043328
+            collective_id=0, has_side_effects=True, vmem_limit_bytes=48 * 1024 * 1024
         ),
-    )(fields, region_label, sheet_shift, diffusivity)
+    )(*(pltpu.with_memory_space_constraint(x, pltpu.HBM) for x in (fields, region_label, sheet_shift, diffusivity)))
     return result[None]
 
 

time: 59.1 us -> 55.9 us (0.946)
  local copies, waits for them, and re-layouts: 3.53 us -> 1.49 us
  Pallas kernels: 55.4 us -> 54.2 us
    unnamed x1, local copies, waits for them, and re-layouts: 3.53 us -> 1.49 us
    pallas_call x1, Pallas kernels: 55.4 us -> 54.2 us  [shards(): pl.pallas_call(kernel, out_shape=jax.ShapeDtypeStruct(fields.shape, f32),...]
where the time goes in v3:
time: 55.9 us; the launch traced here: 55.7 us
  Pallas kernels  54.2 us (97%)
  local copies, waits for them, and re-layouts  1.49 us (3%)
    pallas_call x1, Pallas kernels, shards(): pl.pallas_call(kernel, out_shape=jax.ShapeDtypeStruct(fields.shape, f32),...  54.2 us
    unnamed x1, local copies, waits for them, and re-layouts  1.49 us

profile of v3, /device:TPU:6, one launch (start us, length us, event | category | flops | bytes accessed | tf_op | source)
XLA Modules:
  0.0 55.7 jit_solution(18303394290851269321)
XLA Ops:
  0.0 54.2 %shard_map.46 = f32[5,8,128,128]{3,2,1,0:T(8,128)S(1)} custom-call(f32[5,8,128,128]{3,2,1,0:T(8,128)} %bitcast.3, s32[8,128,128]{2,1,0:T(8,128)} %label_in.1, s32[1,128]{1,0:T(1,128)} %shift_in.1, f32[4]{0:T(128)} %table_in.1), custom_call_target="tpu_custom_call" | custom-call | tf_op jit(solution)/shard_map/pallas_call | solution.py:430
  54.2 1.5 %copy.6 = f32[1,5,8,128,128]{4,3,2,1,0:T(8,128)} copy(f32[1,5,8,128,128]{4,3,2,1,0:T(8,128)S(1)} %bitcast.2) | data formatting | bytes 5242880

commit v4 on v3

--- a/solution.py
+++ b/solution.py
@@ -302,6 +302,16 @@
     body_hop = time_hop(3, ahead, delta)
     up_hop = time_hop(4, ahead.at[depth_c - 1], below.at[0], 1)
     down_hop = time_hop(5, ahead.at[0], below.at[1], -1)
+    start_hop.wait_recv()
+
+    def combine_start(z, r, chunk):
+        at = pl.ds(r, chunk)
+        total = (slice_length * float(INTEGRALS[0, 0])) * start[z, at]
+        for node in range(1, NODES):
+            total = total + (slice_length * float(INTEGRALS[0, node])) * fields[node, z, at]
+        fill(2, z, r, total)
+
+    pl.when(has_prev)(lambda: edges(combine_start))
     lift_hop.wait_recv()
     gain[...] = gain[...] + moved[...]
     body_hop.wait_recv()
@@ -332,8 +342,6 @@
             spread[0, zc, pl.ds(k, rows_c, stride=BLOCK_X)] = delta[zc]
             spread[1, zc, pl.ds(k, rows_c, stride=BLOCK_X)] = ahead[zc]
 
-    start_hop.wait_recv()
-
     @pl.when(jnp.logical_not(has_prev))
     def _():
         def turn(z, carry):
@@ -341,6 +349,15 @@
             return carry
 
         lax.fori_loop(0, depth, turn, 0)
+        edges(combine_start)
+
+    late = slice_length * float((INTEGRALS[0] * TIMES).sum())
+    early = slice_length * float(INTEGRALS[0].sum()) - late
+
+    def correct_edge(z, r, chunk):
+        at, zc = pl.ds(r, chunk), z // BLOCK_Z
+        base = pads[2, z + 1, pl.ds(PAD + r, chunk)]
+        fill(2, z, r, base + (early * spread[0, zc, at] + late * spread[1, zc, at]))
 
     def correct(z, r, chunk):
         at = pl.ds(r, chunk)
@@ -361,10 +378,12 @@
                 values[node - 1, z, at] = value
             term = (slice_length * float(INTEGRALS[0, node])) * value
             total = term if total is None else total + term
-        fill(2, z, r, total)
+        if not isinstance(z, int):
+            fill(2, z, r, total)
 
     pair = halo(2)
-    edges(correct, None, pair)
+    edges(correct_edge, None, pair)
+    edges(correct)
     interior(correct)
 
     for sweep in range(FINE_SWEEPS):

time: 55.9 us -> 55.9 us (level)
  no operation moved by 1% of the time
where the time goes in v4:
time: 55.9 us; the launch traced here: 55.7 us
  Pallas kernels  54.2 us (97%)
  local copies, waits for them, and re-layouts  1.49 us (3%)
    pallas_call x1, Pallas kernels, shards(): pl.pallas_call(kernel, out_shape=jax.ShapeDtypeStruct(fields.shape, f32),...  54.2 us
    unnamed x1, local copies, waits for them, and re-layouts  1.49 us

profile of v4, /device:TPU:6, one launch (start us, length us, event | category | flops | bytes accessed | tf_op | source)
XLA Modules:
  0.0 55.7 jit_solution(14022481530276309879)
XLA Ops:
  0.0 54.2 %shard_map.46 = f32[5,8,128,128]{3,2,1,0:T(8,128)S(1)} custom-call(f32[5,8,128,128]{3,2,1,0:T(8,128)} %bitcast.3, s32[8,128,128]{2,1,0:T(8,128)} %label_in.1, s32[1,128]{1,0:T(1,128)} %shift_in.1, f32[4]{0:T(128)} %table_in.1), custom_call_target="tpu_custom_call" | custom-call | tf_op jit(solution)/shard_map/pallas_call | solution.py:449
  54.2 1.5 %copy.6 = f32[1,5,8,128,128]{4,3,2,1,0:T(8,128)} copy(f32[1,5,8,128,128]{4,3,2,1,0:T(8,128)S(1)} %bitcast.2) | data formatting | bytes 5242880
